TPU v7x, 32 devices: a whole 2x2x4 slice. The times are simulated.
32 devices in a mesh: leaf: 8 (over z, y), sub: 4 (over x, core).
Axes of the slice: x: 2, y: 2, z: 4, core: 2. Of those that a mesh axis runs over, the one named last changes fastest.
Arguments:
- sources: bfloat16 [65536, 64], P(('leaf', 'sub')), may hold values from -6 to 6
- leaf_basis: bfloat16 [256, 256, 64], P(('leaf', 'sub')), may hold values from -0.375 to 0.375
- transfer: float32 [2, 64, 64], replicated, may hold values from -0.625 to 0.625
- coupling: float32 [3, 64, 64], replicated, may hold values from -0.5 to 0.5
- near_blocks: bfloat16 [256, 4, 256, 256], P(('leaf', 'sub')), may hold values from -0.1875 to 0.1875
- near_pattern: int32 [256, 4], P(('leaf', 'sub')), may hold values from 0 to 255, as said below
- far_pattern: int32 [508, 3], replicated, may hold values 0 or 1
Outputs:
- product: bfloat16 [65536, 64], P(('leaf', 'sub'))
Inputs may be any that keep to these rules, and one draw needn't show every extreme that they name: near_pattern[i, 0] = i; every entry j has j // 8 - i // 8 equal to 0, 1, -1, 4 or -4.
All inputs are finite; a program needn't handle non-finite values.
Results may differ from a plain program's by a relative error of at most 0.001.
Values may be sent and summed in bfloat16 or wider, within the bound.
A program may use at most 64 MiB of HBM per device.

v0:
```python
import jax
import jax.numpy as jnp
from jax import lax
from jax.sharding import PartitionSpec as P

PRECISE = lax.Precision.HIGHEST


def padded(block, sides, width):
    for axis, dim in sides:
        count = lax.axis_size(axis)
        forward = [(i, i + 1) for i in range(count - 1)]
        backward = [(target, source) for source, target in forward]
        low = lax.ppermute(
            lax.slice_in_dim(block, block.shape[dim] - width, None, axis=dim), axis, forward
        )
        high = lax.ppermute(lax.slice_in_dim(block, 0, width, axis=dim), axis, backward)
        block = jnp.concatenate([low, block, high], axis=dim)
    return block


def swapped(array, axis, distance):
    return lax.ppermute(array, axis, [(i, i ^ 1 << distance) for i in range(lax.axis_size(axis))])


def lift_up(level_vals, transfer):
    paired = level_vals.reshape(-1, 2, level_vals.shape[1], level_vals.shape[2])
    left_part = jnp.einsum("jk,pjr->pkr", transfer[0], paired[:, 0], precision=PRECISE)
    right_part = jnp.einsum("jk,pjr->pkr", transfer[1], paired[:, 1], precision=PRECISE)
    return left_part + right_part


def expand_down(parent_field, transfer):
    first_child = jnp.einsum("kj,pjr->pkr", transfer[0], parent_field, precision=PRECISE)
    second_child = jnp.einsum("kj,pjr->pkr", transfer[1], parent_field, precision=PRECISE)
    stacked = jnp.stack([first_child, second_child], 1)
    return stacked.reshape(-1, parent_field.shape[1], parent_field.shape[2])


def couple_level(level_vals, mask_rows, coupling):
    grouped = level_vals.reshape(-1, 4, level_vals.shape[1], level_vals.shape[2])
    summed = jnp.zeros(level_vals.shape, jnp.float32)
    for offset in range(1, 4):
        shifted = jnp.roll(grouped, -offset, axis=1).reshape(level_vals.shape)
        product_term = jnp.einsum("ab,nbr->nar", coupling[offset - 1], shifted, precision=PRECISE)
        weights = mask_rows[:, offset - 1 : offset].astype(jnp.float32)[:, :, None]
        summed = summed + weights * product_term
    return summed


def level_share(whole_group, far_pattern, row_start, first_own, own_count, coupling):
    group_start = first_own // 4 * 4
    mask_rows = lax.dynamic_slice_in_dim(far_pattern, row_start + group_start, 4, 0)
    coupled = couple_level(whole_group, mask_rows, coupling)
    return lax.dynamic_slice_in_dim(coupled, first_own % 4, own_count, 0)


def shards(sources, leaf_basis, transfer, coupling, near_blocks, near_pattern, far_pattern):
    leaf_dev = leaf_basis.shape[0]
    leaf_points = leaf_basis.shape[1]
    rhs_width = sources.shape[1]
    device_total = lax.axis_size(("leaf", "sub"))
    device = lax.axis_index(("leaf", "sub"))
    sub_span = lax.axis_size("sub")
    bit_count = device_total.bit_length() - 1
    rows_dev = leaf_dev * leaf_points
    joined = padded(sources, ((("leaf", "sub"), 0),), rows_dev)
    leafwise = padded(sources, (("leaf", 0),), rows_dev)
    buffer = jnp.concatenate([leafwise[:rows_dev], joined, leafwise[2 * rows_dev :]], 0)
    buffer = buffer.reshape(5 * leaf_dev, leaf_points, rhs_width)
    device_gap = near_pattern // leaf_dev - device
    slot_block = jnp.where(
        device_gap == -sub_span,
        0,
        jnp.where(
            device_gap == -1, 1, jnp.where(device_gap == 0, 2, jnp.where(device_gap == 1, 3, 4))
        ),
    )
    gathered = buffer[slot_block * leaf_dev + near_pattern % leaf_dev]
    near_part = jnp.einsum(
        "lsab,lsbr->lar", near_blocks, gathered, preferred_element_type=jnp.float32
    )
    points = sources.reshape(leaf_dev, leaf_points, rhs_width)
    upward = [jnp.einsum("lpk,lpr->lkr", leaf_basis, points, preferred_element_type=jnp.float32)]
    while upward[-1].shape[0] > 1:
        upward.append(lift_up(upward[-1], transfer))
    local_depth = len(upward) - 1
    total_leaves = leaf_dev * device_total
    top_level = local_depth + bit_count - 2
    row_starts = [0]
    for level_id in range(top_level):
        row_starts.append(row_starts[-1] + (total_leaves >> level_id))
    locals_list = []
    for level_id in range(local_depth - 1):
        level_vals = upward[level_id]
        cluster_count = level_vals.shape[0]
        mask_rows = lax.dynamic_slice_in_dim(
            far_pattern, row_starts[level_id] + device * cluster_count, cluster_count, 0
        )
        locals_list.append(couple_level(level_vals, mask_rows, coupling))
    cross_local = {}
    half_group = upward[local_depth - 1]
    for bit_id in range(bit_count):
        partner_half = swapped(half_group, ("leaf", "sub"), bit_id)
        upper_side = device >> bit_id & 1
        whole_group = jnp.where(
            upper_side == 1,
            jnp.concatenate([partner_half, half_group], 0),
            jnp.concatenate([half_group, partner_half], 0),
        )
        level_id = local_depth - 1 + bit_id
        first_own = device * leaf_dev >> level_id
        own_count = 2 if bit_id == 0 else 1
        cross_local[level_id] = level_share(
            whole_group, far_pattern, row_starts[level_id], first_own, own_count, coupling
        )
        if bit_id + 1 < bit_count:
            own_parent = lift_up(half_group, transfer)
            sibling = lift_up(partner_half, transfer)
            half_group = jnp.where(
                upper_side == 1,
                jnp.concatenate([sibling, own_parent], 0),
                jnp.concatenate([own_parent, sibling], 0),
            )
    field_down = cross_local[top_level]
    for level_id in range(top_level - 1, local_depth - 1, -1):
        position = device * leaf_dev >> level_id & 1
        chosen = lax.dynamic_index_in_dim(transfer, position, 0, keepdims=False)
        field_down = cross_local[level_id] + jnp.einsum(
            "kj,pjr->pkr", chosen, field_down, precision=PRECISE
        )
    field_down = cross_local[local_depth - 1] + expand_down(field_down, transfer)
    for level_id in range(local_depth - 2, -1, -1):
        field_down = locals_list[level_id] + expand_down(field_down, transfer)
    far_part = jnp.einsum(
        "lpk,lkr->lpr", leaf_basis.astype(jnp.float32), field_down, precision=PRECISE
    )
    return (far_part + near_part).reshape(rows_dev, rhs_width).astype(jnp.bfloat16)


def solution(mesh):
    placed = (
        P(("leaf", "sub"), None),
        P(("leaf", "sub"), None, None),
        P(),
        P(),
        P(("leaf", "sub"), None, None, None),
        P(("leaf", "sub"), None),
        P(),
    )
    return jax.shard_map(
        shards, mesh=mesh, in_specs=placed, out_specs=P(("leaf", "sub"), None), check_vma=False
    )
```

profile of v0, /device:TPU:0, one launch (start us, length us, event | category | flops | bytes accessed | tf_op | source)
XLA Modules:
  0.0 67.3 jit_solution(14663348474335903255)
XLA Ops:
  0.0 5.0 %collective-permute-start.5 = (bf16[2048,64]{0,1:T(8,128)(2,1)}, bf16[2048,64]{0,1:T(8,128)(2,1)S(1)}, u32[]{:S(2)}, u32[]{:S(2)}) collective-permute-start(bf16[2048,64]{0,1:T(8,128)(2,1)} %param.7), channel_id=1, source_target_pairs={{0,4},{4,8},{8,12},{12,16},{16,20},{20,24},{24,28},{1,5},{5,9},{9,... | collective-permute-start | bytes 786440 | tf_op jit(solution)/shard_map/ppermute | solution.py:14
  5.0 1.5 %collective-permute-start.6 = (bf16[2048,64]{0,1:T(8,128)(2,1)}, bf16[2048,64]{0,1:T(8,128)(2,1)S(1)}, u32[]{:S(2)}, u32[]{:S(2)}) collective-permute-start(bf16[2048,64]{0,1:T(8,128)(2,1)} %param.7), channel_id=1, source_target_pairs={{0,1},{1,2},{2,3},{3,4},{4,5},{5,6},{6,7},{7,8},{8,9},{9,10},{10,1... | collective-permute-start | bytes 786440 | tf_op jit(solution)/shard_map/ppermute | solution.py:14
  6.5 1.3 %collective-permute-start.7 = (bf16[2048,64]{0,1:T(8,128)(2,1)}, bf16[2048,64]{0,1:T(8,128)(2,1)S(1)}, u32[]{:S(2)}, u32[]{:S(2)}) collective-permute-start(bf16[2048,64]{0,1:T(8,128)(2,1)} %param.7), channel_id=1, source_target_pairs={{1,0},{2,1},{3,2},{4,3},{5,4},{6,5},{7,6},{8,7},{9,8},{10,9},{11,1... | collective-permute-start | bytes 786440 | tf_op jit(solution)/shard_map/ppermute | solution.py:17
  7.8 1.3 %collective-permute-start.8 = (bf16[2048,64]{0,1:T(8,128)(2,1)}, bf16[2048,64]{0,1:T(8,128)(2,1)S(1)}, u32[]{:S(2)}, u32[]{:S(2)}) collective-permute-start(bf16[2048,64]{0,1:T(8,128)(2,1)} %param.7), channel_id=1, source_target_pairs={{4,0},{8,4},{12,8},{16,12},{20,16},{24,20},{28,24},{5,1},{9,5},{13... | collective-permute-start | bytes 786440 | tf_op jit(solution)/shard_map/ppermute | solution.py:17
  9.1 1.2 %fusion.18 = f32[8,64,64]{2,1,0:T(8,128)S(1)} fusion(bf16[8,256,64]{1,2,0:T(8,128)(2,1)S(1)} %copy-done, bf16[8,8,8,256]{3,2,1,0:T(8,128)(2,1)} %bitcast.468), kind=kOutput, calls=%fused_computation.47 | convolution fusion | flops 16777216 | bytes 655360 | tf_op jit(solution)/shard_map/lpk,lpr->lkr/dot_general | solution.py:84
  10.3 1.1 %fusion.21 = f32[4,64,64]{2,1,0:T(8,128)S(1)} fusion(f32[4,2,64,64]{3,2,1,0:T(8,128)S(1)} %bitcast.457, f32[2,64,64]{2,1,0:T(8,128)} %param.9), kind=kOutput, calls=%fused_computation.56 | convolution fusion | flops 12582912 | bytes 229376 | tf_op jit(solution)/shard_map/jk,pjr->pkr/dot_general | solution.py:28
  11.5 1.1 %convolution_add_fusion.1 = f32[4,64,64]{2,1,0:T(8,128)S(1)} fusion(f32[4,64,64]{2,1,0:T(8,128)S(1)} %fusion.21, f32[4,2,64,64]{3,2,1,0:T(8,128)S(1)} %bitcast.458, f32[2,64,64]{2,1,0:T(8,128)} %param.9), kind=kOutput, calls=%fused_computation.18 | convolution fusion | flops 12599296 | bytes 360448 | tf_op jit(solution)/shard_map/jk,pjr->pkr/dot_general | solution.py:29
  13.0 2.7 %collective-permute-start = (f32[2,64,64]{1,2,0:T(8,128)S(1)}, f32[2,64,64]{1,2,0:T(8,128)S(1)}, u32[]{:S(2)}, u32[]{:S(2)}) collective-permute-start(f32[2,64,64]{1,2,0:T(8,128)S(1)} %bitcast.473), channel_id=1, source_target_pairs={{0,1},{1,0},{2,3},{3,2},{4,5},{5,4},{6,7},{7,6},{8,9},{9,8},{10,11... | collective-permute-start | bytes 98312 | tf_op jit(solution)/shard_map/ppermute | solution.py:23
  21.7 0.6 dynamic-slice.23
  22.9 0.6 dynamic-slice.21
  24.7 0.6 dynamic-slice.18
  27.0 1.9 %collective-permute-start.1 = (f32[2,64,64]{1,2,0:T(8,128)S(1)}, f32[2,64,64]{1,2,0:T(8,128)S(1)}, u32[]{:S(2)}, u32[]{:S(2)}) collective-permute-start(f32[2,64,64]{1,2,0:T(8,128)S(1)} %maximum_select_fusion.5), channel_id=1, source_target_pairs={{0,2},{1,3},{2,0},{3,1},{4,6},{5,7},{6,4},{7,5},{8,10},{9,11},{10,... | collective-permute-start | bytes 98312 | tf_op jit(solution)/shard_map/ppermute | solution.py:23
  29.7 1.7 %collective-permute-done.1 = f32[2,64,64]{1,2,0:T(8,128)S(1)} collective-permute-done((f32[2,64,64]{1,2,0:T(8,128)S(1)}, f32[2,64,64]{1,2,0:T(8,128)S(1)}, u32[]{:S(2)}, u32[]{:S(2)}) %collective-permute-start.1) | collective-permute-done | bytes 32800 | tf_op jit(solution)/shard_map/ppermute | solution.py:23
  32.2 3.4 %collective-permute-start.2 = (f32[2,64,64]{1,2,0:T(8,128)S(1)}, f32[2,64,64]{1,2,0:T(8,128)S(1)}, u32[]{:S(2)}, u32[]{:S(2)}) collective-permute-start(f32[2,64,64]{1,2,0:T(8,128)S(1)} %maximum_select_fusion.7), channel_id=1, source_target_pairs={{0,4},{1,5},{2,6},{3,7},{4,0},{5,1},{6,2},{7,3},{8,12},{9,13},{10,... | collective-permute-start | bytes 98312 | tf_op jit(solution)/shard_map/ppermute | solution.py:23
  36.5 1.4 %collective-permute-done.2 = f32[2,64,64]{1,2,0:T(8,128)S(1)} collective-permute-done((f32[2,64,64]{1,2,0:T(8,128)S(1)}, f32[2,64,64]{1,2,0:T(8,128)S(1)}, u32[]{:S(2)}, u32[]{:S(2)}) %collective-permute-start.2) | collective-permute-done | bytes 32800 | tf_op jit(solution)/shard_map/ppermute | solution.py:23
  38.3 3.5 %collective-permute-start.3 = (f32[2,64,64]{1,2,0:T(8,128)S(1)}, f32[2,64,64]{1,2,0:T(8,128)S(1)}, u32[]{:S(2)}, u32[]{:S(2)}) collective-permute-start(f32[2,64,64]{1,2,0:T(8,128)S(1)} %maximum_select_fusion.9), channel_id=1, source_target_pairs={{0,8},{1,9},{2,10},{3,11},{4,12},{5,13},{6,14},{7,15},{8,0},{9,1},... | collective-permute-start | bytes 98312 | tf_op jit(solution)/shard_map/ppermute | solution.py:23
  43.0 1.1 %collective-permute-done.3 = f32[2,64,64]{1,2,0:T(8,128)S(1)} collective-permute-done((f32[2,64,64]{1,2,0:T(8,128)S(1)}, f32[2,64,64]{1,2,0:T(8,128)S(1)}, u32[]{:S(2)}, u32[]{:S(2)}) %collective-permute-start.3) | collective-permute-done | bytes 32800 | tf_op jit(solution)/shard_map/ppermute | solution.py:23
  44.5 3.3 %collective-permute-start.4 = (f32[2,64,64]{1,2,0:T(8,128)S(1)}, f32[2,64,64]{1,2,0:T(8,128)S(1)}, u32[]{:S(2)}, u32[]{:S(2)}) collective-permute-start(f32[2,64,64]{1,2,0:T(8,128)S(1)} %maximum_select_fusion.11), channel_id=1, source_target_pairs={{0,16},{1,17},{2,18},{3,19},{4,20},{5,21},{6,22},{7,23},{8,24},{9,... | collective-permute-start | bytes 98312 | tf_op jit(solution)/shard_map/ppermute | solution.py:23
  48.6 1.4 %collective-permute-done.4 = f32[2,64,64]{1,2,0:T(8,128)S(1)} collective-permute-done((f32[2,64,64]{1,2,0:T(8,128)S(1)}, f32[2,64,64]{1,2,0:T(8,128)S(1)}, u32[]{:S(2)}, u32[]{:S(2)}) %collective-permute-start.4) | collective-permute-done | bytes 32800 | tf_op jit(solution)/shard_map/ppermute | solution.py:23
  51.0 4.0 %fusion.13 = f32[64,64]{0,1:T(8,128)S(1)} fusion(f32[4,64,64]{2,1,0:T(8,128)S(1)} %fusion.70, s32[]{:T(128)S(6)} %select_n.320, f32[4,64,64]{2,1,0:T(8,128)S(1)} %fusion.67, f32[4,64,64]{2,1,0:T(8,128)S(1)} %fusion.64, f32[4,64,64]{2,1,0:T(8,128)S(1)} %fusion.61, s32[]{:T(128)S(6)} %select_n.310, f32[4,64,64]{2,1,0:T(8,128)S(1)} %fusion.58, ...), kind=kOutput, calls=%fused_computation.42 | convolution fusion | flops 3190784 | bytes 245796 | tf_op jit(solution)/shard_map/kj,pjr->pkr/dot_general | solution.py:129
  54.9 1.9 %fusion.15 = f32[64,64]{0,1:T(8,128)S(1)} fusion(f32[64,64]{0,1:T(8,128)S(1)} %fusion.13, f32[4,64,64]{2,1,0:T(8,128)S(1)} %fusion.52, s32[]{:T(128)S(6)} %select_n.300, f32[4,64,64]{2,1,0:T(8,128)S(1)} %fusion.49, f32[4,64,64]{2,1,0:T(8,128)S(1)} %fusion.46, f32[2,64,64]{2,1,0:T(8,128)S(1)} %copy-done.1, s32[]{:T(128)S(6)} %select_n.322, ...), kind=kOutput, calls=%fused_computation.44 | convolution fusion | flops 3170304 | bytes 180244 | tf_op jit(solution)/shard_map/kj,pjr->pkr/dot_general | solution.py:129
  56.8 2.1 %fusion.17 = f32[64,64]{0,1:T(8,128)S(1)} fusion(f32[64,64]{0,1:T(8,128)S(1)} %fusion.15, f32[4,64,64]{2,1,0:T(8,128)S(1)} %fusion.43, s32[]{:T(128)S(6)} %select_n.290, f32[4,64,64]{2,1,0:T(8,128)S(1)} %fusion.40, f32[4,64,64]{2,1,0:T(8,128)S(1)} %fusion.37, f32[2,64,64]{2,1,0:T(8,128)S(1)} %copy-done.1, s32[]{:T(128)S(6)} %select_n.323, ...), kind=kOutput, calls=%fused_computation.46 | convolution fusion | flops 3170304 | bytes 180244 | tf_op jit(solution)/shard_map/kj,pjr->pkr/dot_general | solution.py:129
  62.7 3.6 %convolution_bitcast_fusion = f32[8,64,256]{2,1,0:T(8,128)S(1)} fusion(bf16[8,4,256,64]{2,3,1,0:T(8,128)(2,1)S(1)} %bitcast.455, bf16[8,4,256,256]{3,2,1,0:T(8,128)(2,1)} %param.11), kind=kOutput, calls=%fused_computation.2 | convolution fusion | flops 268435456 | bytes 5767168 | tf_op jit(solution)/shard_map/lsab,lsbr->lar/dot_general | solution.py:80
  66.6 0.7 %copy.47 = bf16[8,8,8,256]{3,2,0,1:T(8,128)(2,1)} copy(bf16[8,8,8,256]{3,2,1,0:T(8,128)(2,1)S(1)} %fusion.1) | data formatting | bytes 524288 | tf_op jit(solution)/shard_map/convert_element_type | solution.py:138
  (137 shorter events, 19.0 us)
Async XLA Ops:
  0.0 9.1 %copy-start = (bf16[8,256,64]{1,2,0:T(8,128)(2,1)S(1)}, bf16[8,256,64]{1,2,0:T(8,128)(2,1)}, u32[]{:S(2)}) copy-start(bf16[8,256,64]{1,2,0:T(8,128)(2,1)} %param.8) | copy-start | bytes 786436
  0.0 12.6 %copy-start.1 = (f32[2,64,64]{2,1,0:T(8,128)S(1)}, f32[2,64,64]{2,1,0:T(8,128)}, u32[]{:S(2)}) copy-start(f32[2,64,64]{2,1,0:T(8,128)} %param.9) | copy-start | bytes 98308
  0.0 61.6 %collective-permute-start.5 = (bf16[2048,64]{0,1:T(8,128)(2,1)}, bf16[2048,64]{0,1:T(8,128)(2,1)S(1)}, u32[]{:S(2)}, u32[]{:S(2)}) collective-permute-start(bf16[2048,64]{0,1:T(8,128)(2,1)} %param.7), channel_id=1, source_target_pairs={{0,4},{4,8},{8,12},{12,16},{16,20},{20,24},{24,28},{1,5},{5,9},{9,... | collective-permute-start | bytes 786440 | tf_op jit(solution)/shard_map/ppermute | solution.py:14
  5.0 56.6 %collective-permute-start.6 = (bf16[2048,64]{0,1:T(8,128)(2,1)}, bf16[2048,64]{0,1:T(8,128)(2,1)S(1)}, u32[]{:S(2)}, u32[]{:S(2)}) collective-permute-start(bf16[2048,64]{0,1:T(8,128)(2,1)} %param.7), channel_id=1, source_target_pairs={{0,1},{1,2},{2,3},{3,4},{4,5},{5,6},{6,7},{7,8},{8,9},{9,10},{10,1... | collective-permute-start | bytes 786440 | tf_op jit(solution)/shard_map/ppermute | solution.py:14
  6.5 55.3 %collective-permute-start.7 = (bf16[2048,64]{0,1:T(8,128)(2,1)}, bf16[2048,64]{0,1:T(8,128)(2,1)S(1)}, u32[]{:S(2)}, u32[]{:S(2)}) collective-permute-start(bf16[2048,64]{0,1:T(8,128)(2,1)} %param.7), channel_id=1, source_target_pairs={{1,0},{2,1},{3,2},{4,3},{5,4},{6,5},{7,6},{8,7},{9,8},{10,9},{11,1... | collective-permute-start | bytes 786440 | tf_op jit(solution)/shard_map/ppermute | solution.py:17
  7.8 54.0 %collective-permute-start.8 = (bf16[2048,64]{0,1:T(8,128)(2,1)}, bf16[2048,64]{0,1:T(8,128)(2,1)S(1)}, u32[]{:S(2)}, u32[]{:S(2)}) collective-permute-start(bf16[2048,64]{0,1:T(8,128)(2,1)} %param.7), channel_id=1, source_target_pairs={{4,0},{8,4},{12,8},{16,12},{20,16},{24,20},{28,24},{5,1},{9,5},{13... | collective-permute-start | bytes 786440 | tf_op jit(solution)/shard_map/ppermute | solution.py:17
  12.8 3.1 %copy-start.5 = (s32[8,4]{0,1:T(4,128)S(1)}, s32[8,4]{0,1:T(4,128)}, u32[]{:S(2)}) copy-start(s32[8,4]{0,1:T(4,128)} %param.12) | copy-start | bytes 388
  13.0 13.2 %collective-permute-start = (f32[2,64,64]{1,2,0:T(8,128)S(1)}, f32[2,64,64]{1,2,0:T(8,128)S(1)}, u32[]{:S(2)}, u32[]{:S(2)}) collective-permute-start(f32[2,64,64]{1,2,0:T(8,128)S(1)} %bitcast.473), channel_id=1, source_target_pairs={{0,1},{1,0},{2,3},{3,2},{4,5},{5,4},{6,7},{7,6},{8,9},{9,8},{10,11... | collective-permute-start | bytes 98312 | tf_op jit(solution)/shard_map/ppermute | solution.py:23
  15.8 0.8 %copy-start.4 = (s32[508,3]{0,1:T(4,128)S(1)}, s32[508,3]{0,1:T(4,128)}, u32[]{:S(2)}) copy-start(s32[508,3]{0,1:T(4,128)} %param.13) | copy-start | bytes 18292
  15.9 1.0 %copy-start.2 = (f32[3,64,64]{2,1,0:T(8,128)S(1)}, f32[3,64,64]{2,1,0:T(8,128)}, u32[]{:S(2)}) copy-start(f32[3,64,64]{2,1,0:T(8,128)} %param.10) | copy-start | bytes 147460
  27.0 4.5 %collective-permute-start.1 = (f32[2,64,64]{1,2,0:T(8,128)S(1)}, f32[2,64,64]{1,2,0:T(8,128)S(1)}, u32[]{:S(2)}, u32[]{:S(2)}) collective-permute-start(f32[2,64,64]{1,2,0:T(8,128)S(1)} %maximum_select_fusion.5), channel_id=1, source_target_pairs={{0,2},{1,3},{2,0},{3,1},{4,6},{5,7},{6,4},{7,5},{8,10},{9,11},{10,... | collective-permute-start | bytes 98312 | tf_op jit(solution)/shard_map/ppermute | solution.py:23
  32.2 5.6 %collective-permute-start.2 = (f32[2,64,64]{1,2,0:T(8,128)S(1)}, f32[2,64,64]{1,2,0:T(8,128)S(1)}, u32[]{:S(2)}, u32[]{:S(2)}) collective-permute-start(f32[2,64,64]{1,2,0:T(8,128)S(1)} %maximum_select_fusion.7), channel_id=1, source_target_pairs={{0,4},{1,5},{2,6},{3,7},{4,0},{5,1},{6,2},{7,3},{8,12},{9,13},{10,... | collective-permute-start | bytes 98312 | tf_op jit(solution)/shard_map/ppermute | solution.py:23
  38.3 5.8 %collective-permute-start.3 = (f32[2,64,64]{1,2,0:T(8,128)S(1)}, f32[2,64,64]{1,2,0:T(8,128)S(1)}, u32[]{:S(2)}, u32[]{:S(2)}) collective-permute-start(f32[2,64,64]{1,2,0:T(8,128)S(1)} %maximum_select_fusion.9), channel_id=1, source_target_pairs={{0,8},{1,9},{2,10},{3,11},{4,12},{5,13},{6,14},{7,15},{8,0},{9,1},... | collective-permute-start | bytes 98312 | tf_op jit(solution)/shard_map/ppermute | solution.py:23
  44.5 5.5 %collective-permute-start.4 = (f32[2,64,64]{1,2,0:T(8,128)S(1)}, f32[2,64,64]{1,2,0:T(8,128)S(1)}, u32[]{:S(2)}, u32[]{:S(2)}) collective-permute-start(f32[2,64,64]{1,2,0:T(8,128)S(1)} %maximum_select_fusion.11), channel_id=1, source_target_pairs={{0,16},{1,17},{2,18},{3,19},{4,20},{5,21},{6,22},{7,23},{8,24},{9,... | collective-permute-start | bytes 98312 | tf_op jit(solution)/shard_map/ppermute | solution.py:23
  60.8 1.0 %copy-start.3 = (bf16[2048,64]{0,1:T(8,128)(2,1)S(1)}, bf16[2048,64]{0,1:T(8,128)(2,1)}, u32[]{:S(2)}) copy-start(bf16[2048,64]{0,1:T(8,128)(2,1)} %param.7) | copy-start | bytes 786436
where the time goes:
time: 67.9 us; the launch traced here: 67.3 us
  matrix products  26.1 us (38%)
  starting transfers between devices  24 us (35%)
  local copies, waits for them, and re-layouts  10.1 us (15%)
  waiting for transfers between devices  5.63 us (8%)
  between operations  1.18 us (2%)
    ppermute x5, starting transfers between devices, swapped(): lax.ppermute(array, axis, [(i, i ^ 1 << distance) for i in range(lax.axis...  14.9 us
    dot_general x3, matrix products, shards(): jnp.einsum('kj,pjr->pkr', chosen, field_down, precision=PRECISE)  7.95 us
    ppermute x2, starting transfers between devices, padded(): lax.ppermute(lax.slice_in_dim(block, block.shape[dim] - width, None, axis...  6.51 us
    dot_general x21, matrix products, couple_level(): jnp.einsum('ab,nbr->nar', coupling[offset - 1], shifted, precision=PRECISE)  6.48 us
    ppermute x5, waiting for transfers between devices, swapped(): lax.ppermute(array, axis, [(i, i ^ 1 << distance) for i in range(lax.axis...  5.62 us
    dynamic_slice x9, local copies, waits for them, and re-layouts, level_share(): return lax.dynamic_slice_in_dim(coupled, first_own % 4, own_count, 0)  5.46 us
    dot_general x1, matrix products, shards(): jnp.einsum('lsab,lsbr->lar', near_blocks, gathered, preferred_element_typ...  3.56 us
    dot_general x10, matrix products, lift_up(): jnp.einsum('jk,pjr->pkr', transfer[0], paired[:, 0], precision=PRECISE)  2.64 us
  transfers between devices with their start and end apart: 9, of which 4 were waited for; matrix products, arithmetic and copies ran while one was open for 46% of the time, Pallas kernels for 0%

commit v1 on v0

v1 whole, which is shorter than its diff:
```python
import functools

import jax
import jax.numpy as jnp
from jax import lax
from jax.experimental import pallas as pl
from jax.experimental.pallas import tpu as pltpu
from jax.sharding import PartitionSpec as P

BF = jnp.bfloat16
F32 = jnp.float32
MESH = pl.DeviceIdType.MESH


def halves(x):
    hi = x.astype(BF)
    return hi, (x - hi.astype(F32)).astype(BF)


def split(x):
    return jnp.concatenate(halves(x), axis=1)


def nt(a, b):
    return lax.dot_general(a, b, (((1,), (1,)), ((), ())), preferred_element_type=F32)


def nn(a, b):
    return jnp.dot(a, b, preferred_element_type=F32)


def fold(y, width):
    return y[:, :width] + y[:, width:]


def kernel(
    cfg, src, basis, transfer, coupling, blocks, near_pat, far_pat, out,
    buf, bas, nb, buf_a, pair2, buf4, buf5, buf6, wdown,
    load_sem, nb_sem, halo_send, halo_recv, a_send, a_recv, p_send, p_recv,
    b_send, b_recv, q_send, q_recv,
):
    sub, devices, leaf_dev, near = cfg
    rank = basis.shape[1]
    rhs = src.shape[0]
    points = basis.shape[2]
    block = 2 * sub
    block_count = devices // block
    me = lax.axis_index("leaf") * sub + lax.axis_index("sub")
    mine = lax.rem(me, block)
    own_block = me // block

    def target(dev):
        return (dev // sub, lax.rem(dev, sub))

    loads = [
        pltpu.make_async_copy(
            src.at[:, pl.ds(points * leaf, points)], buf.at[2, leaf], load_sem.at[leaf]
        )
        for leaf in range(leaf_dev)
    ]
    base_load = pltpu.make_async_copy(basis, bas, load_sem.at[leaf_dev])
    for copy in loads:
        copy.start()
    base_load.start()
    near_loads = [
        pltpu.make_async_copy(blocks.at[leaf], nb.at[leaf], nb_sem.at[leaf])
        for leaf in range(leaf_dev)
    ]
    for copy in near_loads:
        copy.start()

    barrier = pltpu.get_barrier_semaphore()
    steps = (-sub, -1, 1, sub)

    def present(step):
        return me + step >= 0 if step < 0 else me + step < devices

    peers = []
    for k in range(1, block):
        peers.append(own_block * block + lax.rem(mine + k, block))
    for k in range(1, block_count):
        peers.append(lax.rem(own_block + k, block_count) * block + mine)
    for peer in peers:
        pl.semaphore_signal(barrier, inc=1, device_id=target(peer), device_id_type=MESH)
    expected = len(peers)
    for step in steps:
        outside = present(step) & (lax.rem(me + step + devices, devices) // block != own_block)
        expected = expected + jnp.where(outside, 1, 0)

        @pl.when(outside)
        def _(step=step):
            pl.semaphore_signal(barrier, inc=1, device_id=target(me + step), device_id_type=MESH)
    thi, tlo = [], []
    for side in range(2):
        hi, lo = halves(transfer[side])
        thi.append(hi)
        tlo.append(lo)
    up_rows = []
    for side in range(2):
        row = jnp.concatenate([thi[side], tlo[side]], axis=1)
        up_rows += [row, row]
    w_up = jnp.concatenate(up_rows, axis=0)
    for side in range(2):
        wdown[side] = jnp.concatenate(
            [
                jnp.concatenate([thi[side], thi[side]], axis=1),
                jnp.concatenate([tlo[side], tlo[side]], axis=1),
            ],
            axis=0,
        )
    c_hi, c_lo = [], []
    for offset in range(3):
        hi, lo = halves(coupling[offset])
        c_hi += [hi, hi]
        c_lo += [lo, lo]
    w_couple = jnp.concatenate(
        [jnp.concatenate(c_hi, axis=1), jnp.concatenate(c_lo, axis=1)], axis=0
    )

    def lift(rows):
        return split(fold(nn(rows, w_up), rank))

    def pairs(split_vals, count):
        top = [
            jnp.concatenate(
                [
                    split_vals[2 * p * rhs : (2 * p + 1) * rhs],
                    split_vals[(2 * p + 1) * rhs : (2 * p + 2) * rhs],
                ],
                axis=1,
            )
            for p in range(count)
        ]
        return top[0] if count == 1 else jnp.concatenate(top, axis=0)

    pl.semaphore_wait(barrier, expected)
    for number, step in enumerate(steps):
        @pl.when(present(step))
        def _(step=step, number=number):
            slot = len(steps) - number if number < 2 else 3 - number
            for leaf in range(leaf_dev):
                pltpu.make_async_remote_copy(
                    src_ref=src.at[:, pl.ds(points * leaf, points)],
                    dst_ref=buf.at[slot, leaf],
                    send_sem=halo_send.at[number],
                    recv_sem=halo_recv.at[3 - number],
                    device_id=target(me + step),
                    device_id_type=MESH,
                ).start()

    for copy in loads:
        copy.wait()
    base_load.wait()
    moment0 = jnp.concatenate(
        [nt(buf[2, leaf], bas[leaf]) for leaf in range(leaf_dev)], axis=0
    )
    levels = [split(moment0)]
    count = leaf_dev
    while count > 2:
        count //= 2
        levels.append(lift(pairs(levels[-1], count)))
    two = pairs(levels[-1], 1)
    pair2[0] = two

    def remote(source, dest, send, recv, dev):
        return pltpu.make_async_remote_copy(
            src_ref=source, dst_ref=dest, send_sem=send, recv_sem=recv,
            device_id=target(dev), device_id_type=MESH,
        )

    sibling = me + 1 - 2 * lax.rem(me, 2)
    pair_copy = remote(pair2.at[0], pair2.at[1], p_send.at[0], p_recv.at[0], sibling)
    pair_copy.start()
    buf_a[mine] = lift(two)
    a_copies = []
    for k in range(1, block):
        a_copies.append(
            remote(
                buf_a.at[mine], buf_a.at[mine], a_send.at[k], a_recv.at[k],
                own_block * block + lax.rem(mine + k, block),
            )
        )
    for copy in a_copies:
        copy.start()

    row_starts = [0]
    total = leaf_dev * devices
    size = total
    while size > 4:
        row_starts.append(row_starts[-1] + size)
        size //= 2

    def weight(offset, row):
        return jnp.full((rhs, 2 * rank), far_pat[offset, row].astype(F32), F32).astype(BF)

    def couple(groups, rows):
        stacked = [
            jnp.concatenate(
                [weight(offset, row) * members[offset] for offset in range(3)], axis=1
            )
            for members, row in zip(groups, rows)
        ]
        stacked = stacked[0] if len(stacked) == 1 else jnp.concatenate(stacked, axis=0)
        return fold(nt(stacked, w_couple), rank)

    locals_low = []
    level_id = 0
    while (leaf_dev >> level_id) >= 4:
        vals = levels[level_id]
        count = leaf_dev >> level_id
        parts = [vals[c * rhs : (c + 1) * rhs] for c in range(count)]
        groups = [
            [parts[c // 4 * 4 + (c + offset) % 4] for offset in range(1, 4)] for c in range(count)
        ]
        rows = [row_starts[level_id] + me * count + c for c in range(count)]
        locals_low.append(couple(groups, rows))
        level_id += 1
    for copy in near_loads:
        copy.wait()
    first = [nt(buf[2, leaf], nb[leaf, 0]) for leaf in range(leaf_dev)]

    pair_copy.wait()
    other = pair2[1]
    members2 = [
        two[:, : 2 * rank], two[:, 2 * rank :], other[:, : 2 * rank], other[:, 2 * rank :]
    ]
    locals_low.append(
        couple(
            [[members2[(c + offset) % 4] for offset in range(1, 4)] for c in range(2)],
            [row_starts[level_id] + me * 2 + c for c in range(2)],
        )
    )
    level_id += 1

    for k in range(1, block):
        source = lax.rem(mine - k + block, block)
        remote(
            buf_a.at[source], buf_a.at[source], a_send.at[k], a_recv.at[k], me ^ 1
        ).wait_recv()
    quarter = block // 2
    four = lift(
        jnp.concatenate(
            [jnp.concatenate([buf_a[2 * p], buf_a[2 * p + 1]], axis=1) for p in range(quarter)],
            axis=0,
        )
    )
    for p in range(quarter):
        buf4[p] = four[p * rhs : (p + 1) * rhs]
    five = lift(pairs(four, 2))
    for p in range(2):
        buf5[p] = five[p * rhs : (p + 1) * rhs]
    buf6[own_block] = lift(pairs(five, 1))
    partner_block = own_block + 1 - 2 * lax.rem(own_block, 2)
    q_copy = remote(
        buf5.at[pl.ds(0, 2)], buf5.at[pl.ds(2, 2)], q_send.at[0], q_recv.at[0],
        partner_block * block + mine,
    )
    b_copies = []
    for k in range(1, block_count):
        b_copies.append(
            remote(
                buf6.at[own_block], buf6.at[own_block], b_send.at[k], b_recv.at[k],
                lax.rem(own_block + k, block_count) * block + mine,
            )
        )
    for copy in b_copies:
        copy.start()
    q_copy.start()

    base = mine // sub * sub
    place = lax.rem(me, sub)
    groups = [[buf_a[base + lax.rem(place + offset, 4)] for offset in range(1, 4)]]
    rows = [row_starts[level_id] + me]
    place = mine // 2
    groups.append([buf4[lax.rem(place + offset, 4)] for offset in range(1, 4)])
    rows.append(row_starts[level_id + 1] + me // 2)
    both = couple(groups, rows)
    locals_high = [both[:rhs], both[rhs:]]

    for k in range(1, block_count):
        source = lax.rem(own_block - k + block_count, block_count)
        remote(
            buf6.at[source], buf6.at[source], b_send.at[k], b_recv.at[k], me ^ 1
        ).wait_recv()
    q_copy.wait()
    place = mine // sub
    groups = [[buf5[lax.rem(place + offset, 4)] for offset in range(1, 4)]]
    rows = [row_starts[level_id + 2] + me // 4]
    first_six = level_id + 3
    groups.append(
        [
            buf6[own_block // 4 * 4 + lax.rem(lax.rem(own_block, 4) + offset, 4)]
            for offset in range(1, 4)
        ]
    )
    rows.append(row_starts[first_six] + own_block)
    start, span, level = 0, block_count, first_six
    while span > 4:
        above = lift(
            jnp.concatenate(
                [
                    jnp.concatenate([buf6[start + 2 * p], buf6[start + 2 * p + 1]], axis=1)
                    for p in range(span // 2)
                ],
                axis=0,
            )
        )
        for p in range(span // 2):
            buf6[start + span + p] = above[p * rhs : (p + 1) * rhs]
        start, span, level = start + span, span // 2, level + 1
        own = own_block >> (level - first_six)
        groups.append(
            [
                buf6[start + own // 4 * 4 + lax.rem(lax.rem(own, 4) + offset, 4)]
                for offset in range(1, 4)
            ]
        )
        rows.append(row_starts[level] + own)
    top = couple(groups, rows)
    locals_high += [top[p * rhs : (p + 1) * rhs] for p in range(len(groups))]

    field = locals_high[-1]
    for step in range(len(locals_high) - 2, -1, -1):
        parity = lax.rem(me >> step, 2)
        field = locals_high[step] + fold(nt(split(field), wdown[parity]), rank)
    w_down = jnp.concatenate([wdown[0], wdown[1]], axis=0)
    count = 1
    for step in range(len(locals_low) - 1, -1, -1):
        both = nt(split(field), w_down)
        children = []
        for p in range(count):
            row = both[p * rhs : (p + 1) * rhs]
            children.append(fold(row[:, : 2 * rank], rank))
            children.append(fold(row[:, 2 * rank :], rank))
        field = locals_low[step] + jnp.concatenate(children, axis=0)
        count *= 2
    spread = split(field)
    partial = []
    for leaf in range(leaf_dev):
        doubled = jnp.concatenate([bas[leaf], bas[leaf]], axis=0)
        partial.append(first[leaf] + nn(spread[leaf * rhs : (leaf + 1) * rhs], doubled))

    for number, step in enumerate(steps):
        @pl.when(present(step))
        def _(number=number):
            slot = number if number < 2 else number + 1
            pltpu.make_async_copy(buf.at[slot], buf.at[slot], halo_recv.at[number]).wait()
    for leaf in range(leaf_dev):
        acc = partial[leaf]
        for s in range(1, near):
            index = near_pat[s, leaf]
            gap = index // leaf_dev - me
            place = jnp.where(
                gap == -sub, 0, jnp.where(gap == -1, 1, jnp.where(gap == 0, 2, jnp.where(gap == 1, 3, 4)))
            )
            acc = acc + nt(buf[place, lax.rem(index, leaf_dev)], nb[leaf, s])
        out[:, points * leaf : points * (leaf + 1)] = acc.astype(out.dtype)

    for number, step in enumerate(steps):
        @pl.when(present(step))
        def _(number=number):
            pltpu.make_async_copy(buf.at[2], buf.at[2], halo_send.at[number]).wait()
    for copy in a_copies + b_copies:
        copy.wait_send()


def shards(sizes, sources, leaf_basis, transfer, coupling, near_blocks, near_pattern, far_pattern):
    sub, devices = sizes
    leaf_dev, points, rank = leaf_basis.shape
    rhs = sources.shape[1]
    near = near_blocks.shape[1]
    block = 2 * sub
    block_count = devices // block
    vmem = pl.BlockSpec(memory_space=pltpu.VMEM)
    smem = pl.BlockSpec(memory_space=pltpu.SMEM)
    hbm = pl.BlockSpec(memory_space=pl.ANY)
    dma = pltpu.SemaphoreType.DMA
    result = pl.pallas_call(
        functools.partial(kernel, (sub, devices, leaf_dev, near)),
        out_shape=jax.ShapeDtypeStruct((rhs, leaf_dev * points), BF),
        in_specs=[hbm, hbm, vmem, vmem, hbm, smem, smem],
        out_specs=vmem,
        scratch_shapes=[
            pltpu.VMEM((5, leaf_dev, rhs, points), BF),
            pltpu.VMEM((leaf_dev, rank, points), BF),
            pltpu.VMEM((leaf_dev, near, points, points), BF),
            pltpu.VMEM((block, rhs, 2 * rank), BF),
            pltpu.VMEM((2, rhs, 4 * rank), BF),
            pltpu.VMEM((4, rhs, 2 * rank), BF),
            pltpu.VMEM((4, rhs, 2 * rank), BF),
            pltpu.VMEM((2 * block_count, rhs, 2 * rank), BF),
            pltpu.VMEM((2, 2 * rank, 2 * rank), BF),
            dma((leaf_dev + 1,)),
            dma((leaf_dev,)),
            dma((4,)),
            dma((4,)),
            dma((block,)),
            dma((block,)),
            dma((1,)),
            dma((1,)),
            dma((block_count,)),
            dma((block_count,)),
            dma((1,)),
            dma((1,)),
        ],
        compiler_params=pltpu.CompilerParams(collective_id=0, has_side_effects=True),
    )(
        sources.T,
        leaf_basis.transpose(0, 2, 1),
        transfer,
        coupling,
        near_blocks,
        near_pattern.T,
        far_pattern.T,
    )
    return result.T


def solution(mesh):
    placed = (
        P(("leaf", "sub"), None),
        P(("leaf", "sub"), None, None),
        P(),
        P(),
        P(("leaf", "sub"), None, None, None),
        P(("leaf", "sub"), None),
        P(),
    )
    sizes = (mesh.shape["sub"], mesh.shape["leaf"] * mesh.shape["sub"])
    return jax.shard_map(
        functools.partial(shards, sizes),
        mesh=mesh, in_specs=placed, out_specs=P(("leaf", "sub"), None), check_vma=False,
    )
```

time: 67.9 us -> 34.7 us (0.51)
  Pallas kernels: 0 us -> 32.8 us
  matrix products: 26.1 us -> 0 us
  starting transfers between devices: 24 us -> 0 us
  local copies, waits for them, and re-layouts: 10.1 us -> 1.67 us
  waiting for transfers between devices: 5.63 us -> 0 us
  between operations: 1.18 us -> 0.01 us
    pallas_call x0 -> x1, Pallas kernels: none -> 32.8 us  [shards(): pl.pallas_call(functools.partial(kernel, (sub, devices, leaf_dev, near)),...]
    dot_general x53 -> x0, matrix products: 26.1 us -> none  [the longest x3 7.95 us: shards(): jnp.einsum('kj,pjr->pkr', chosen, field_down, precision=PRECISE)]
    ppermute x9 -> x0, starting transfers between devices: 24 us -> none  [the longest x5 14.9 us: swapped(): lax.ppermute(array, axis, [(i, i ^ 1 << distance) for i in range(lax.axis...]
    ppermute x9 -> x0, waiting for transfers between devices: 5.63 us -> none  [the longest x5 5.62 us: swapped(): lax.ppermute(array, axis, [(i, i ^ 1 << distance) for i in range(lax.axis...]
    dynamic_slice x11 -> x0, local copies, waits for them, and re-layouts: 5.62 us -> none  [the longest x9 5.46 us: level_share(): return lax.dynamic_slice_in_dim(coupled, first_own % 4, own_count, 0)]
    another operation x8 -> x0, local copies, waits for them, and re-layouts: 2.15 us -> none
    unnamed x16 -> x1, local copies, waits for them, and re-layouts: 0.23 us -> 1.67 us
    convert_element_type x1 -> x0, local copies, waits for them, and re-layouts: 0.72 us -> none  [shards(): (far_part + near_part).reshape(rows_dev, rhs_width).astype(jnp.bfloat16)]
  transfers between devices with their start and end apart: 9 -> 0, of which waited for: 4 -> 0; matrix products, arithmetic and copies ran while one was open for 46% -> 0% of each run, Pallas kernels for 0% -> 0%
where the time goes in v1:
time: 34.7 us; the launch traced here: 34.5 us
  Pallas kernels  32.8 us (95%)
  local copies, waits for them, and re-layouts  1.67 us (5%)
    pallas_call x1, Pallas kernels, shards(): pl.pallas_call(functools.partial(kernel, (sub, devices, leaf_dev, near)),...  32.8 us
    unnamed x1, local copies, waits for them, and re-layouts  1.67 us

profile of v1, /device:TPU:0, one launch (start us, length us, event | category | flops | bytes accessed | tf_op | source)
XLA Modules:
  0.0 34.5 jit_solution(6748380670450781773)
XLA Ops:
  0.0 32.8 %shard_map.73 = bf16[64,2048]{1,0:T(8,128)(2,1)} custom-call(bf16[64,2048]{1,0:T(8,128)(2,1)} %bitcast.6, bf16[8,64,256]{2,1,0:T(8,128)(2,1)} %bitcast.7, f32[2,64,64]{2,1,0:T(8,128)} %transfer.1, f32[3,64,64]{2,1,0:T(8,128)} %coupling.1, bf16[8,4,256,256]{3,2,1,0:T(8,128)(2,1)} %blocks.1, s32[4,8]{1,0:T(4,128)} %bitcast.9, s32[3,508]{1,0:T(4,128)} %bitcast.8), custom_call_target="tpu_custom_call" | custom-call | tf_op jit(solution)/shard_map/pallas_call | solution.py:378
  32.9 1.7 %copy.9 = bf16[2048,64]{0,1:T(8,128)(2,1)} copy(bf16[2048,64]{0,1:T(8,128)(2,1)} %bitcast.5) | data formatting | bytes 524288

commit v2 on v1

v2 whole, which is shorter than its diff:
```python
import functools

import jax
import jax.numpy as jnp
from jax import lax
from jax.experimental import pallas as pl
from jax.experimental.pallas import tpu as pltpu
from jax.sharding import PartitionSpec as P

BF = jnp.bfloat16
F32 = jnp.float32
MESH = pl.DeviceIdType.MESH


def halves(x):
    hi = x.astype(BF)
    return hi, (x - hi.astype(F32)).astype(BF)


def split(x):
    return jnp.concatenate(halves(x), axis=1)


def nt(a, b):
    return lax.dot_general(a, b, (((1,), (1,)), ((), ())), preferred_element_type=F32)


def nn(a, b):
    return jnp.dot(a, b, preferred_element_type=F32)


def fold(y, width):
    return y[:, :width] + y[:, width:]


def kernel(
    cfg, src, basis, transfer, coupling, blocks, near_pat, far_pat, out,
    buf, bas, nb, buf_a, pair2, buf4, buf5, buf6, wdown, wpath,
    load_sem, nb_sem, halo_send, near_recv, y_recv, z_recv, a_send, a_recv, p_send, p_recv,
    b_send, b_recv, q_send, q_recv,
):
    sub, devices, leaf_dev, near = cfg
    rank = basis.shape[1]
    rhs = src.shape[0]
    points = basis.shape[2]
    block = 2 * sub
    block_count = devices // block
    me = lax.axis_index("leaf") * sub + lax.axis_index("sub")
    mine = lax.rem(me, block)
    own_block = me // block
    place_sub = lax.rem(me, sub)
    upper = mine // sub

    def target(dev):
        return (dev // sub, lax.rem(dev, sub))

    def remote(source, dest, send, recv, dev):
        return pltpu.make_async_remote_copy(
            src_ref=source, dst_ref=dest, send_sem=send, recv_sem=recv,
            device_id=target(dev), device_id_type=MESH,
        )

    barrier = pltpu.get_barrier_semaphore()
    peers = []
    for k in range(1, block_count):
        peers.append(lax.rem(own_block + k, block_count) * block + mine)
    for k in range(1, block):
        peers.append(own_block * block + lax.rem(mine + k, block))
    for peer in peers:
        pl.semaphore_signal(barrier, inc=1, device_id=target(peer), device_id_type=MESH)

    loads = [
        pltpu.make_async_copy(
            src.at[:, pl.ds(points * leaf, points)], buf.at[2, leaf], load_sem.at[leaf]
        )
        for leaf in range(leaf_dev)
    ]
    base_load = pltpu.make_async_copy(basis, bas, load_sem.at[leaf_dev])
    base_load.start()
    for copy in loads:
        copy.start()
    near_loads = [
        pltpu.make_async_copy(blocks.at[leaf], nb.at[leaf], nb_sem.at[leaf])
        for leaf in range(leaf_dev)
    ]
    for copy in near_loads:
        copy.start()

    def doubled(parts):
        rows = []
        for part in parts:
            row = split(part)
            rows += [row, row]
        return jnp.concatenate(rows, axis=0)

    sides = [transfer[side] for side in range(2)]
    step_weight = jnp.concatenate([doubled([side]) for side in sides], axis=1)
    w_up = {2: doubled(sides)}
    paths = sides
    while len(paths) < max(leaf_dev, block):
        wide = nn(split(jnp.concatenate(paths, axis=0)), step_weight)
        longer = jnp.concatenate(
            [fold(wide[:, : 2 * rank], rank), fold(wide[:, 2 * rank :], rank)], axis=0
        )
        paths = [longer[p * rank : (p + 1) * rank] for p in range(2 * len(paths))]
        w_up[len(paths)] = doubled(paths)

    def lift(parts, span):
        rows = [
            jnp.concatenate(parts[p * span : (p + 1) * span], axis=1)
            for p in range(len(parts) // span)
        ]
        rows = rows[0] if len(rows) == 1 else jnp.concatenate(rows, axis=0)
        lifted = split(fold(nn(rows, w_up[span]), rank))
        return [lifted[p * rhs : (p + 1) * rhs] for p in range(len(parts) // span)]

    base_load.wait()
    moment0 = []
    for leaf in range(leaf_dev):
        loads[leaf].wait()
        moment0.append(split(nt(buf[2, leaf], bas[leaf])))
    buf_a[mine] = lift(moment0, leaf_dev)[0]
    two = lift(moment0, leaf_dev // 2)
    pair2[0, 0] = two[0]
    pair2[0, 1] = two[1]

    pl.semaphore_wait(barrier, len(peers))
    a_copies = []
    for k in range(block - 1, 0, -1):
        a_copies.append(
            remote(
                buf_a.at[mine], buf_a.at[mine], a_send.at[k], a_recv.at[k],
                own_block * block + lax.rem(mine + k, block),
            )
        )
    for copy in a_copies:
        copy.start()
    pair_copy = remote(
        pair2.at[0], pair2.at[1], p_send.at[0], p_recv.at[0], me + 1 - 2 * lax.rem(me, 2)
    )
    pair_copy.start()

    y_slot = 4 - 4 * upper
    z_slot = 4 * upper
    across = me + sub - 2 * sub * upper
    for leaf in range(leaf_dev):
        remote(
            src.at[:, pl.ds(points * leaf, points)], buf.at[z_slot, leaf],
            halo_send.at[0], y_recv.at[leaf], across,
        ).start()
    for number, step in enumerate((1, -1)):
        @pl.when(place_sub < sub - 1 if step > 0 else place_sub > 0)
        def _(number=number, step=step):
            for leaf in range(leaf_dev):
                remote(
                    src.at[:, pl.ds(points * leaf, points)], buf.at[2 - step, leaf],
                    halo_send.at[1 + number], near_recv.at[number], me + step,
                ).start()

    z_step = block - 2 * block * upper
    z_target = me + z_step
    z_send = (z_target >= 0) & (z_target < devices)
    z_have = (me - z_step >= 0) & (me - z_step < devices)
    first_turn = ((upper == 0) & (place_sub == 0)) | ((upper == 1) & (place_sub == sub - 1))
    second_turn = z_have & (
        ((upper == 0) & (place_sub == sub - 1)) | ((upper == 1) & (place_sub == 0))
    )

    def turn(slot, leaf):
        @pl.when(place_sub == 0)
        def _():
            remote(
                buf.at[slot, leaf], buf.at[3, leaf],
                halo_send.at[4], near_recv.at[1], me + sub - 1,
            ).start()

        @pl.when(place_sub == sub - 1)
        def _():
            remote(
                buf.at[slot, leaf], buf.at[1, leaf],
                halo_send.at[4], near_recv.at[0], me - sub + 1,
            ).start()

    def relay_first(leaf):
        remote(
            buf.at[y_slot, leaf], buf.at[y_slot, leaf], halo_send.at[0], y_recv.at[leaf], across
        ).wait_recv()

        @pl.when(z_send)
        def _():
            remote(
                buf.at[y_slot, leaf], buf.at[z_slot, leaf],
                halo_send.at[3], z_recv.at[leaf], z_target,
            ).start()

        @pl.when(first_turn)
        def _():
            turn(y_slot, leaf)

    def z_wait(leaf):
        remote(
            buf.at[z_slot, leaf], buf.at[z_slot, leaf], halo_send.at[3], z_recv.at[leaf], across
        ).wait_recv()

    def relay_second(leaf):
        @pl.when(second_turn)
        def _():
            z_wait(leaf)
            turn(z_slot, leaf)

    row_starts = [0]
    size = leaf_dev * devices
    while size > 4:
        row_starts.append(row_starts[-1] + size)
        size //= 2

    def weight(offset, row):
        return jnp.full((rhs, 2 * rank), far_pat[offset, row].astype(F32), F32).astype(BF)

    c_hi, c_lo = [], []
    for offset in range(3):
        hi, lo = halves(coupling[offset])
        c_hi += [hi, hi]
        c_lo += [lo, lo]
    w_couple = jnp.concatenate(
        [jnp.concatenate(c_hi, axis=1), jnp.concatenate(c_lo, axis=1)], axis=0
    )

    def couple(groups, rows):
        stacked = [
            jnp.concatenate(
                [weight(offset, row) * members[offset] for offset in range(3)], axis=1
            )
            for members, row in zip(groups, rows)
        ]
        stacked = stacked[0] if len(stacked) == 1 else jnp.concatenate(stacked, axis=0)
        return fold(nt(stacked, w_couple), rank)

    for side in range(2):
        hi, lo = halves(sides[side])
        wdown[side] = jnp.concatenate(
            [jnp.concatenate([hi, hi], axis=1), jnp.concatenate([lo, lo], axis=1)], axis=0
        )
    w_down = jnp.concatenate([wdown[0], wdown[1]], axis=0)

    def descend(field, step):
        return fold(nt(split(field), wdown[lax.rem(me >> step, 2)]), rank)

    def fan_out(field, rows):
        both = nt(split(field), w_down)
        children = []
        for p in range(field.shape[0] // rows):
            row = both[p * rows : (p + 1) * rows]
            children.append(fold(row[:, : 2 * rank], rank))
            children.append(fold(row[:, 2 * rank :], rank))
        return jnp.concatenate(children, axis=0)

    low_levels = leaf_dev.bit_length() - 1
    top_count = len(row_starts) - low_levels - 2
    eye = (
        lax.broadcasted_iota(jnp.int32, (rank, rank), 0)
        == lax.broadcasted_iota(jnp.int32, (rank, rank), 1)
    ).astype(F32)
    chain = eye
    for step in range(top_count, -1, -1):
        if step <= 1:
            chain = descend(chain, step)
        elif step < top_count + 1:
            chain = jnp.concatenate([descend(chain, step), eye], axis=0)
    for _ in range(low_levels):
        chain = fan_out(chain, top_count * rank)
    for leaf in range(leaf_dev):
        for number in range(top_count):
            begin = (leaf * top_count + number) * rank
            piece = split(chain[begin : begin + rank])
            for half in range(2):
                wpath[
                    (2 * number + half) * rank : (2 * number + half + 1) * rank,
                    2 * rank * leaf : 2 * rank * (leaf + 1),
                ] = piece

    locals_low = []
    level_vals, level_id = moment0, 0
    while (leaf_dev >> level_id) >= 4:
        if level_id:
            level_vals = lift(level_vals, 2)
        count = leaf_dev >> level_id
        locals_low.append(
            couple(
                [
                    [level_vals[c // 4 * 4 + (c + offset) % 4] for offset in range(1, 4)]
                    for c in range(count)
                ],
                [row_starts[level_id] + me * count + c for c in range(count)],
            )
        )
        level_id += 1

    for k in range(block - 1, 0, -1):
        source = lax.rem(mine - k + block, block)
        remote(
            buf_a.at[source], buf_a.at[source], a_send.at[k], a_recv.at[k], me ^ 1
        ).wait_recv()
    eight = [buf_a[p] for p in range(block)]
    buf6[own_block] = lift(eight, block)[0]
    b_copies = []
    for k in range(block_count - 1, 0, -1):
        b_copies.append(
            remote(
                buf6.at[own_block], buf6.at[own_block], b_send.at[k], b_recv.at[k],
                lax.rem(own_block + k, block_count) * block + mine,
            )
        )
    for copy in b_copies:
        copy.start()
    five = lift(eight, block // 2)
    for p in range(2):
        buf5[p] = five[p]
    q_copy = remote(
        buf5.at[pl.ds(0, 2)], buf5.at[pl.ds(2, 2)], q_send.at[0], q_recv.at[0],
        (own_block + 1 - 2 * lax.rem(own_block, 2)) * block + mine,
    )
    q_copy.start()
    relay_first(0)
    relay_first(1)
    for p, part in enumerate(lift(eight, 2)):
        buf4[p] = part

    pair_copy.wait()
    members2 = two + [pair2[1, 0], pair2[1, 1]]
    groups = [[members2[(c + offset) % 4] for offset in range(1, 4)] for c in range(2)]
    rows = [row_starts[level_id] + me * 2 + c for c in range(2)]
    level_id += 1
    groups.append(
        [buf_a[upper * sub + lax.rem(place_sub + offset, 4)] for offset in range(1, 4)]
    )
    rows.append(row_starts[level_id] + me)
    groups.append([buf4[lax.rem(mine // 2 + offset, 4)] for offset in range(1, 4)])
    rows.append(row_starts[level_id + 1] + me // 2)
    relay_first(2)
    middle = couple(groups, rows)
    locals_low.append(middle[: 2 * rhs])
    relay_first(3)
    field = middle[2 * rhs : 3 * rhs] + descend(middle[3 * rhs :], 0)
    for step in range(len(locals_low) - 1, -1, -1):
        field = locals_low[step] + fan_out(field, rhs)
    relay_first(4)

    for copy in near_loads:
        copy.wait()
    first = [nt(buf[2, leaf], nb[leaf, 0]) for leaf in range(leaf_dev)]
    for leaf in range(5, leaf_dev):
        relay_first(leaf)
    for leaf in range(leaf_dev):
        relay_second(leaf)

    for k in range(block_count - 1, 0, -1):
        source = lax.rem(own_block - k + block_count, block_count)
        remote(
            buf6.at[source], buf6.at[source], b_send.at[k], b_recv.at[k], me ^ 1
        ).wait_recv()
    q_copy.wait()
    groups = [[buf5[lax.rem(upper + offset, 4)] for offset in range(1, 4)]]
    rows = [row_starts[level_id + 2] + me // sub]
    first_six = level_id + 3
    start, span, level = 0, block_count, first_six
    while True:
        own = own_block >> (level - first_six)
        groups.append(
            [
                buf6[start + own // 4 * 4 + lax.rem(lax.rem(own, 4) + offset, 4)]
                for offset in range(1, 4)
            ]
        )
        rows.append(row_starts[level] + own)
        if span <= 4:
            break
        for p, part in enumerate(lift([buf6[start + p] for p in range(span)], 2)):
            buf6[start + span + p] = part
        start, span, level = start + span, span // 2, level + 1
    groups, rows = groups[::-1], rows[::-1]
    top = split(couple(groups, rows))
    top = jnp.concatenate([top[p * rhs : (p + 1) * rhs] for p in range(top_count)], axis=1)
    spread = nn(top, wpath[...])
    partial = []
    for leaf in range(leaf_dev):
        whole = split(
            field[leaf * rhs : (leaf + 1) * rhs]
            + fold(spread[:, 2 * rank * leaf : 2 * rank * (leaf + 1)], rank)
        )
        twice = jnp.concatenate([bas[leaf], bas[leaf]], axis=0)
        partial.append(first[leaf] + nn(whole, twice))

    @pl.when(z_have & jnp.logical_not(second_turn))
    def _():
        for leaf in range(leaf_dev):
            z_wait(leaf)

    for number, step in enumerate((-1, 1)):
        @pl.when(me > 0 if step < 0 else me < devices - 1)
        def _(number=number, step=step):
            pltpu.make_async_copy(buf.at[2 + step], buf.at[2 + step], near_recv.at[number]).wait()
    for leaf in range(leaf_dev):
        acc = partial[leaf]
        for s in range(1, near):
            index = near_pat[s, leaf]
            gap = index // leaf_dev - me
            place = jnp.where(
                gap == -sub, 0, jnp.where(gap == -1, 1, jnp.where(gap == 0, 2, jnp.where(gap == 1, 3, 4)))
            )
            acc = acc + nt(buf[place, lax.rem(index, leaf_dev)], nb[leaf, s])
        out[:, points * leaf : points * (leaf + 1)] = acc.astype(out.dtype)

    sent = (
        me >= 0, place_sub < sub - 1, place_sub > 0, z_send, first_turn | second_turn,
    )
    for number, condition in enumerate(sent):
        @pl.when(condition)
        def _(number=number):
            pltpu.make_async_copy(buf.at[2], buf.at[2], halo_send.at[number]).wait()
    for copy in a_copies + b_copies:
        copy.wait_send()


def shards(sizes, sources, leaf_basis, transfer, coupling, near_blocks, near_pattern, far_pattern):
    sub, devices = sizes
    leaf_dev, points, rank = leaf_basis.shape
    rhs = sources.shape[1]
    near = near_blocks.shape[1]
    block = 2 * sub
    block_count = devices // block
    top_count = block_count.bit_length() - 1
    vmem = pl.BlockSpec(memory_space=pltpu.VMEM)
    smem = pl.BlockSpec(memory_space=pltpu.SMEM)
    hbm = pl.BlockSpec(memory_space=pl.ANY)
    dma = pltpu.SemaphoreType.DMA
    result = pl.pallas_call(
        functools.partial(kernel, (sub, devices, leaf_dev, near)),
        out_shape=jax.ShapeDtypeStruct((rhs, leaf_dev * points), BF),
        in_specs=[hbm, hbm, vmem, vmem, hbm, smem, smem],
        out_specs=vmem,
        scratch_shapes=[
            pltpu.VMEM((5, leaf_dev, rhs, points), BF),
            pltpu.VMEM((leaf_dev, rank, points), BF),
            pltpu.VMEM((leaf_dev, near, points, points), BF),
            pltpu.VMEM((block, rhs, 2 * rank), BF),
            pltpu.VMEM((2, 2, rhs, 2 * rank), BF),
            pltpu.VMEM((4, rhs, 2 * rank), BF),
            pltpu.VMEM((4, rhs, 2 * rank), BF),
            pltpu.VMEM((2 * block_count, rhs, 2 * rank), BF),
            pltpu.VMEM((2, 2 * rank, 2 * rank), BF),
            pltpu.VMEM((2 * top_count * rank, 2 * rank * leaf_dev), BF),
            dma((leaf_dev + 1,)),
            dma((leaf_dev,)),
            dma((5,)),
            dma((2,)),
            dma((leaf_dev,)),
            dma((leaf_dev,)),
            dma((block,)),
            dma((block,)),
            dma((1,)),
            dma((1,)),
            dma((block_count,)),
            dma((block_count,)),
            dma((1,)),
            dma((1,)),
        ],
        compiler_params=pltpu.CompilerParams(collective_id=0, has_side_effects=True),
    )(
        sources.T,
        leaf_basis.transpose(0, 2, 1),
        transfer,
        coupling,
        near_blocks,
        near_pattern.T,
        far_pattern.T,
    )
    return result.T


def solution(mesh):
    placed = (
        P(("leaf", "sub"), None),
        P(("leaf", "sub"), None, None),
        P(),
        P(),
        P(("leaf", "sub"), None, None, None),
        P(("leaf", "sub"), None),
        P(),
    )
    sizes = (mesh.shape["sub"], mesh.shape["leaf"] * mesh.shape["sub"])
    return jax.shard_map(
        functools.partial(shards, sizes),
        mesh=mesh, in_specs=placed, out_specs=P(("leaf", "sub"), None), check_vma=False,
    )
```

time: 34.7 us -> 24.6 us (0.71)
  the two profiles are of different devices: /device:TPU:0 before, /device:TPU:23 now
where the time goes in v2:
time: 24.6 us; the launch traced here: 24.4 us
  Pallas kernels  22.7 us (92%)
  local copies, waits for them, and re-layouts  1.67 us (7%)
    pallas_call x1, Pallas kernels, shards(): pl.pallas_call(functools.partial(kernel, (sub, devices, leaf_dev, near)),...  22.7 us
    unnamed x1, local copies, waits for them, and re-layouts  1.67 us

profile of v2, /device:TPU:23, one launch (start us, length us, event | category | flops | bytes accessed | tf_op | source)
XLA Modules:
  0.0 24.4 jit_solution(6258204074541047445)
XLA Ops:
  0.0 22.7 %shard_map.73 = bf16[64,2048]{1,0:T(8,128)(2,1)} custom-call(bf16[64,2048]{1,0:T(8,128)(2,1)} %bitcast.6, bf16[8,64,256]{2,1,0:T(8,128)(2,1)} %bitcast.7, f32[2,64,64]{2,1,0:T(8,128)} %transfer.1, f32[3,64,64]{2,1,0:T(8,128)} %coupling.1, bf16[8,4,256,256]{3,2,1,0:T(8,128)(2,1)} %blocks.1, s32[4,8]{1,0:T(4,128)} %bitcast.9, s32[3,508]{1,0:T(4,128)} %bitcast.8), custom_call_target="tpu_custom_call" | custom-call | tf_op jit(solution)/shard_map/pallas_call | solution.py:437
  22.7 1.7 %copy.9 = bf16[2048,64]{0,1:T(8,128)(2,1)} copy(bf16[2048,64]{0,1:T(8,128)(2,1)} %bitcast.5) | data formatting | bytes 524288

commit v3 on v2

--- a/solution.py
+++ b/solution.py
@@ -115,10 +115,9 @@
         return [lifted[p * rhs : (p + 1) * rhs] for p in range(len(parts) // span)]
 
     base_load.wait()
-    moment0 = []
-    for leaf in range(leaf_dev):
-        loads[leaf].wait()
-        moment0.append(split(nt(buf[2, leaf], bas[leaf])))
+    for copy in loads:
+        copy.wait()
+    moment0 = [split(nt(buf[2, leaf], bas[leaf])) for leaf in range(leaf_dev)]
     buf_a[mine] = lift(moment0, leaf_dev)[0]
     two = lift(moment0, leaf_dev // 2)
     pair2[0, 0] = two[0]
@@ -143,11 +142,16 @@
     y_slot = 4 - 4 * upper
     z_slot = 4 * upper
     across = me + sub - 2 * sub * upper
-    for leaf in range(leaf_dev):
-        remote(
-            src.at[:, pl.ds(points * leaf, points)], buf.at[z_slot, leaf],
-            halo_send.at[0], y_recv.at[leaf], across,
-        ).start()
+
+    def send_across():
+        for leaf in range(leaf_dev):
+            remote(
+                src.at[:, pl.ds(points * leaf, points)], buf.at[z_slot, leaf],
+                halo_send.at[0], y_recv.at[leaf], across,
+            ).start()
+
+    outer = (place_sub == 0) | (place_sub == sub - 1)
+    pl.when(outer)(send_across)
     for number, step in enumerate((1, -1)):
         @pl.when(place_sub < sub - 1 if step > 0 else place_sub > 0)
         def _(number=number, step=step):
@@ -296,6 +300,8 @@
         )
         level_id += 1
 
+    pl.when(jnp.logical_not(outer))(send_across)
+
     for k in range(block - 1, 0, -1):
         source = lax.rem(mine - k + block, block)
         remote(
@@ -436,7 +442,7 @@
     dma = pltpu.SemaphoreType.DMA
     result = pl.pallas_call(
         functools.partial(kernel, (sub, devices, leaf_dev, near)),
-        out_shape=jax.ShapeDtypeStruct((rhs, leaf_dev * points), BF),
+        out_shape=pltpu.VMEM((rhs, leaf_dev * points), BF),
         in_specs=[hbm, hbm, vmem, vmem, hbm, smem, smem],
         out_specs=vmem,
         scratch_shapes=[

time: 24.6 us -> 22.7 us (0.923)
  the two profiles are of different devices: /device:TPU:23 before, /device:TPU:7 now
where the time goes in v3:
time: 22.7 us; the launch traced here: 22.4 us
  Pallas kernels  21.7 us (96%)
  local copies, waits for them, and re-layouts  0.71 us (3%)
    pallas_call x1, Pallas kernels, shards(): pl.pallas_call(functools.partial(kernel, (sub, devices, leaf_dev, near)),...  21.7 us
    unnamed x1, local copies, waits for them, and re-layouts  0.71 us

profile of v3, /device:TPU:7, one launch (start us, length us, event | category | flops | bytes accessed | tf_op | source)
XLA Modules:
  0.0 22.4 jit_solution(16981357596702520998)
XLA Ops:
  0.0 21.7 %shard_map.73 = bf16[64,2048]{1,0:T(8,128)(2,1)S(1)} custom-call(bf16[64,2048]{1,0:T(8,128)(2,1)} %bitcast.6, bf16[8,64,256]{2,1,0:T(8,128)(2,1)} %bitcast.7, f32[2,64,64]{2,1,0:T(8,128)} %transfer.1, f32[3,64,64]{2,1,0:T(8,128)} %coupling.1, bf16[8,4,256,256]{3,2,1,0:T(8,128)(2,1)} %blocks.1, s32[4,8]{1,0:T(4,128)} %bitcast.9, s32[3,508]{1,0:T(4,128)} %bitcast.8), custom_call_target="tpu_custom_call" | custom-call | tf_op jit(solution)/shard_map/pallas_call | solution.py:443
  21.7 0.7 %copy.9 = bf16[2048,64]{0,1:T(8,128)(2,1)} copy(bf16[2048,64]{0,1:T(8,128)(2,1)S(1)} %bitcast.5) | data formatting | bytes 524288

commit v4 on v3

--- a/solution.py
+++ b/solution.py
@@ -37,7 +37,7 @@
     cfg, src, basis, transfer, coupling, blocks, near_pat, far_pat, out,
     buf, bas, nb, buf_a, pair2, buf4, buf5, buf6, wdown, wpath,
     load_sem, nb_sem, halo_send, near_recv, y_recv, z_recv, a_send, a_recv, p_send, p_recv,
-    b_send, b_recv, q_send, q_recv,
+    b_send, b_recv, q_send, q_recv, known,
 ):
     sub, devices, leaf_dev, near = cfg
     rank = basis.shape[1]
@@ -62,12 +62,33 @@
 
     barrier = pltpu.get_barrier_semaphore()
     peers = []
-    for k in range(1, block_count):
-        peers.append(lax.rem(own_block + k, block_count) * block + mine)
     for k in range(1, block):
         peers.append(own_block * block + lax.rem(mine + k, block))
+
+    def greet(semaphore, condition, peer):
+        @pl.when(condition)
+        def _():
+            pl.semaphore_signal(semaphore, inc=1, device_id=target(peer), device_id_type=MESH)
+
+    greet(barrier, own_block > 0, me - block)
+    greet(barrier, own_block < block_count - 1, me + block)
     for peer in peers:
         pl.semaphore_signal(barrier, inc=1, device_id=target(peer), device_id_type=MESH)
+
+    rounds = block_count - 2
+
+    def make_known(r):
+        greet(known.at[r - 1, 0], (own_block > 0) & (own_block + r < block_count), me - block)
+        greet(known.at[r - 1, 1], (own_block < block_count - 1) & (own_block >= r), me + block)
+
+    def get_known(r):
+        @pl.when(own_block + r + 1 < block_count)
+        def _():
+            pl.semaphore_wait(known.at[r - 1, 0], 1)
+
+        @pl.when(own_block >= r + 1)
+        def _():
+            pl.semaphore_wait(known.at[r - 1, 1], 1)
 
     loads = [
         pltpu.make_async_copy(
@@ -123,7 +144,8 @@
     pair2[0, 0] = two[0]
     pair2[0, 1] = two[1]
 
-    pl.semaphore_wait(barrier, len(peers))
+    ends = jnp.where(own_block > 0, 1, 0) + jnp.where(own_block < block_count - 1, 1, 0)
+    pl.semaphore_wait(barrier, len(peers) + ends)
     a_copies = []
     for k in range(block - 1, 0, -1):
         a_copies.append(
@@ -138,6 +160,9 @@
         pair2.at[0], pair2.at[1], p_send.at[0], p_recv.at[0], me + 1 - 2 * lax.rem(me, 2)
     )
     pair_copy.start()
+
+    if rounds > 0:
+        make_known(1)
 
     y_slot = 4 - 4 * upper
     z_slot = 4 * upper
@@ -283,6 +308,23 @@
                     2 * rank * leaf : 2 * rank * (leaf + 1),
                 ] = piece
 
+    def relays(early, late):
+        @pl.when(outer)
+        def _():
+            for step, leaf in early:
+                step(leaf)
+
+        if late:
+            @pl.when(jnp.logical_not(outer))
+            def _():
+                for leaf in late:
+                    relay_first(leaf)
+
+    queue = [(relay_first, leaf) for leaf in range(leaf_dev)]
+    queue += [(relay_second, leaf) for leaf in range(leaf_dev)]
+    half = leaf_dev // 2
+    relays(queue[:half], [])
+
     locals_low = []
     level_vals, level_id = moment0, 0
     while (leaf_dev >> level_id) >= 4:
@@ -300,7 +342,10 @@
         )
         level_id += 1
 
-    pl.when(jnp.logical_not(outer))(send_across)
+    for r in range(1, rounds + 1):
+        get_known(r)
+        if r < rounds:
+            make_known(r + 1)
 
     for k in range(block - 1, 0, -1):
         source = lax.rem(mine - k + block, block)
@@ -327,8 +372,8 @@
         (own_block + 1 - 2 * lax.rem(own_block, 2)) * block + mine,
     )
     q_copy.start()
-    relay_first(0)
-    relay_first(1)
+    pl.when(jnp.logical_not(outer))(send_across)
+    relays(queue[half:leaf_dev], [])
     for p, part in enumerate(lift(eight, 2)):
         buf4[p] = part
 
@@ -343,22 +388,18 @@
     rows.append(row_starts[level_id] + me)
     groups.append([buf4[lax.rem(mine // 2 + offset, 4)] for offset in range(1, 4)])
     rows.append(row_starts[level_id + 1] + me // 2)
-    relay_first(2)
+    relays(queue[leaf_dev : leaf_dev + 2], range(0, 2))
     middle = couple(groups, rows)
     locals_low.append(middle[: 2 * rhs])
-    relay_first(3)
     field = middle[2 * rhs : 3 * rhs] + descend(middle[3 * rhs :], 0)
     for step in range(len(locals_low) - 1, -1, -1):
         field = locals_low[step] + fan_out(field, rhs)
-    relay_first(4)
+    relays(queue[leaf_dev + 2 : leaf_dev + half], range(2, half))
 
     for copy in near_loads:
         copy.wait()
     first = [nt(buf[2, leaf], nb[leaf, 0]) for leaf in range(leaf_dev)]
-    for leaf in range(5, leaf_dev):
-        relay_first(leaf)
-    for leaf in range(leaf_dev):
-        relay_second(leaf)
+    relays(queue[leaf_dev + half :], range(half, leaf_dev))
 
     for k in range(block_count - 1, 0, -1):
         source = lax.rem(own_block - k + block_count, block_count)
@@ -470,6 +511,7 @@
             dma((block_count,)),
             dma((1,)),
             dma((1,)),
+            pltpu.SemaphoreType.REGULAR((max(block_count - 2, 1), 2)),
         ],
         compiler_params=pltpu.CompilerParams(collective_id=0, has_side_effects=True),
     )(

time: 22.7 us -> 22.3 us (0.982)
  the two profiles are of different devices: /device:TPU:7 before, /device:TPU:23 now
where the time goes in v4:
time: 22.3 us; the launch traced here: 22.1 us
  Pallas kernels  21.3 us (96%)
  local copies, waits for them, and re-layouts  0.71 us (3%)
    pallas_call x1, Pallas kernels, shards(): pl.pallas_call(functools.partial(kernel, (sub, devices, leaf_dev, near)),...  21.3 us
    unnamed x1, local copies, waits for them, and re-layouts  0.71 us

profile of v4, /device:TPU:23, one launch (start us, length us, event | category | flops | bytes accessed | tf_op | source)
XLA Modules:
  0.0 22.1 jit_solution(5065929700500254295)
XLA Ops:
  0.0 21.3 %shard_map.73 = bf16[64,2048]{1,0:T(8,128)(2,1)S(1)} custom-call(bf16[64,2048]{1,0:T(8,128)(2,1)} %bitcast.6, bf16[8,64,256]{2,1,0:T(8,128)(2,1)} %bitcast.7, f32[2,64,64]{2,1,0:T(8,128)} %transfer.1, f32[3,64,64]{2,1,0:T(8,128)} %coupling.1, bf16[8,4,256,256]{3,2,1,0:T(8,128)(2,1)} %blocks.1, s32[4,8]{1,0:T(4,128)} %bitcast.9, s32[3,508]{1,0:T(4,128)} %bitcast.8), custom_call_target="tpu_custom_call" | custom-call | tf_op jit(solution)/shard_map/pallas_call | solution.py:484
  21.3 0.7 %copy.9 = bf16[2048,64]{0,1:T(8,128)(2,1)} copy(bf16[2048,64]{0,1:T(8,128)(2,1)S(1)} %bitcast.5) | data formatting | bytes 524288
